TPU v7x, 512 devices: a whole 4x8x8 slice. The times are simulated.
512 devices in a mesh: dp: 16 (over z, core), cls: 32 (over x, y).
Axes of the slice: x: 4, y: 8, z: 8, core: 2. Of those that a mesh axis runs over, the one named last changes fastest.
Arguments:
- embeddings: bfloat16 [131072, 768], P(('dp', 'cls'))
- class_rows: bfloat16 [128, 256, 768], P('cls')
- cand_blocks: int32 [1024, 8], P(('dp', 'cls')), may hold values from 0 to 127, all different within a row; in each aligned block of 64 rows (0 to 63, 64 to 127, ...) at most 8 rows name the same one
- label_pos: int32 [131072], P(('dp', 'cls')), may hold values from 0 to 2047
Outputs:
- image_loss: float32 [131072], P('dp')
- class_grad: float32 [256, 128, 768], P('dp', 'cls')
Inputs may be any that keep to these rules, and one draw needn't show every extreme that they name: `cand_blocks`: the 8 blocks of one list differ; block n lives on index n // 4 of cls. Among the 64 lists of one index of dp no block is named by more than 8 lists, and in some index of dp one block is named by exactly 8.
All inputs are finite; a program needn't handle non-finite values.
Results may differ from a plain program's by a relative error of at most 0.00099.
Values may be sent and summed in bfloat16 or wider, within the bound.
A program may use at most 64 MiB of HBM per device.

v0:
```python
import jax
import jax.numpy as jnp
from jax import lax
from jax.sharding import PartitionSpec as P

MOST = 8
NEG = -1e30


def body(embeddings, class_rows, cand_blocks, label_pos):
    gathered, cand_all, labels_all = (
        lax.all_gather(embeddings, "cls", axis=0, tiled=True),
        lax.all_gather(cand_blocks, "cls", axis=0, tiled=True),
        lax.all_gather(label_pos, "cls", axis=0, tiled=True),
    )
    local_blocks, block_taxa, feature_width = class_rows.shape
    group_lists = cand_all.shape[0]
    dp_images = gathered.shape[0]
    group_rows = dp_images // group_lists
    my_shard = lax.axis_index("cls")
    owned_ids = my_shard * local_blocks + jnp.arange(local_blocks, dtype=jnp.int32)
    matches = (cand_all[:, :, None] == owned_ids[None, None, :]).astype(jnp.int32)
    hit_count = jnp.sum(matches, axis=1)
    slot_of = jnp.sum(
        matches * jnp.arange(cand_all.shape[1], dtype=jnp.int32)[None, :, None], axis=1
    )
    hit_rank = jnp.cumsum(hit_count, axis=0) - 1
    slot_ids = jnp.arange(MOST, dtype=jnp.int32)
    picked = (
        (hit_count[:, :, None] > 0) & (hit_rank[:, :, None] == slot_ids[None, None, :])
    ).astype(jnp.int32)
    block_index = jnp.arange(group_lists, dtype=jnp.int32)[:, None, None]
    src_block = jnp.sum(picked * block_index, axis=0)
    valid_slot = jnp.sum(picked, axis=0)
    src_slot = jnp.sum(picked * slot_of[:, :, None], axis=0)
    image_tiles = gathered.reshape(group_lists, group_rows, feature_width)[src_block]
    label_tiles = labels_all.reshape(group_lists, group_rows)[src_block]
    scores = jnp.einsum(
        "jsid,jtd->jsit", image_tiles, class_rows, preferred_element_type=jnp.float32
    )
    live_slot = (valid_slot > 0)[:, :, None, None]
    target_pos = (
        src_slot[:, :, None, None] * block_taxa
        + jnp.arange(block_taxa, dtype=jnp.int32)[None, None, None, :]
    )
    is_true = (label_tiles[:, :, :, None] == target_pos) & live_slot
    true_slot = jnp.sum(jnp.where(is_true, scores, 0.0), axis=3)
    slot_max = jnp.max(scores, axis=3)
    owner_map = picked.reshape(group_lists, local_blocks * MOST)
    owner_float = owner_map.astype(jnp.float32)
    flat_max = slot_max.reshape(local_blocks * MOST, group_rows)
    local_max = jnp.max(jnp.where(owner_map[:, :, None] > 0, flat_max[None, :, :], NEG), axis=1)
    local_true = jnp.einsum(
        "bq,qi->bi", owner_float, true_slot.reshape(-1, group_rows), precision=lax.Precision.HIGHEST
    )
    score_max = lax.pmax(local_max.astype(jnp.bfloat16), "cls").astype(local_max.dtype)
    per_slot = score_max[src_block]
    exp_weights = jnp.where(live_slot, jnp.exp(scores - per_slot[:, :, :, None]), 0.0)
    exp_total, true_total = lax.psum(
        (
            jnp.einsum(
                "bq,qi->bi",
                owner_float,
                jnp.sum(exp_weights, axis=3).reshape(-1, group_rows),
                precision=lax.Precision.HIGHEST,
            ),
            local_true,
        ),
        "cls",
    )
    log_norm = score_max + jnp.log(exp_total)
    image_loss = (log_norm - true_total).reshape(dp_images)
    softmax_prob = jnp.exp(scores - log_norm[src_block][:, :, :, None])
    logit_grad = jnp.where(live_slot, softmax_prob - is_true.astype(jnp.float32), 0.0).astype(
        jnp.bfloat16
    )
    row_share = block_taxa // lax.axis_size("dp")
    whole_sum = lax.psum(
        jnp.einsum("jsit,jsid->tjd", logit_grad, image_tiles, preferred_element_type=jnp.float32),
        "dp",
    )
    class_grad = lax.dynamic_slice_in_dim(whole_sum, lax.axis_index("dp") * row_share, row_share, 0)
    return (image_loss, class_grad)


def solution(mesh):
    in_specs = (
        P(("dp", "cls"), None),
        P("cls", None, None),
        P(("dp", "cls"), None),
        P(("dp", "cls")),
    )
    out_specs = (P("dp"), P("dp", "cls", None))
    return jax.shard_map(body, mesh=mesh, in_specs=in_specs, out_specs=out_specs, check_vma=False)
```

profile of v0, /device:TPU:1, one launch (start us, length us, event | category | flops | bytes accessed | tf_op | source)
XLA Modules:
  0.0 591.8 jit_solution(9255299646218935432)
XLA Ops:
  7.2 0.7 all-gather.4.cloned.1.call-update
  8.0 33.4 %all-gather = s32[32,2,8]{2,1,0:T(2,128)S(1)} all-gather(s32[1,2,8]{2,1,0:T(2,128)} %bitcast.56), channel_id=1, replica_groups=mesh['dp'=16,'cls'=32] {'cls'}, dimensions={0}, use_global_device_ids=true | all-gather | bytes 2112 | tf_op jit(solution)/shard_map/all_gather | solution.py:13
  41.4 0.1 copy.26
  41.4 0.1 fusion.10
  41.5 0.1 copy.27
  41.6 0.1 reduce_window_sum.11
  41.7 0.1 copy.28
  41.8 0.3 select_reduce_fusion.3
  42.1 0.1 reshape.114
  42.2 0.1 eq.63
  42.3 0.1 convert_compare_fusion
  42.4 0.1 copy.29
  42.5 30.6 %all-gather.1 = s32[32,1,256]{2,1,0:T(1,128)S(1)} all-gather(s32[1,1,256]{2,1,0:T(1,128)} %bitcast.57), channel_id=1, replica_groups=mesh['dp'=16,'cls'=32] {'cls'}, dimensions={0}, use_global_device_ids=true | all-gather | bytes 33792 | tf_op jit(solution)/shard_map/all_gather | solution.py:14
  73.1 0.6 gather_fusion.2
  73.7 0.1 iota_add_fusion
  73.8 66.1 %all-gather.4.cloned.1.call-done = bf16[8192,768]{1,0:T(8,128)(2,1)} async-done(((bf16[256,768]{1,0:T(8,128)(2,1)}), bf16[8192,768]{1,0:T(8,128)(2,1)}) %all-gather.4.cloned.1.call-update) | async-done | bytes 12582928 | tf_op jit(solution)/shard_map/all_gather | solution.py:12
  139.9 8.1 %gather_fusion = bf16[32,128,768]{2,1,0:T(8,128)(2,1)} fusion(bf16[64,128,768]{2,1,0:T(8,128)(2,1)} %bitcast.48, s32[1024]{0:T(1024)S(1)} %pad_clamp_fusion), kind=kCustom, calls=%fused_computation | custom fusion | bytes 12583040 | tf_op jit(solution)/shard_map/gather | solution.py:36
  148.1 6.5 %fusion.20 = (bf16[4,8,128]{2,1,0:T(8,128)(2,1)S(1)}, f32[4,8,128,256]{3,2,1,0:T(8,128)}) fusion(bf16[4,8,128,768]{3,2,1,0:T(8,128)(2,1)} %bitcast.46, bf16[4,256,768]{2,1,0:T(8,128)(2,1)S(1)} %copy-done), kind=kOutput, calls=%fused_computation.49 | convolution fusion | flops 1611657216 | bytes 12066816 | tf_op jit(solution)/shard_map/jsid,jtd->jsit/dot_general | solution.py:38
  154.6 0.4 select_reduce_fusion.2
  155.0 111.6 %pmax.7 = bf16[64,128]{1,0:T(8,128)(2,1)S(1)} all-reduce(bf16[64,128]{1,0:T(8,128)(2,1)S(1)} %select_reduce_fusion.2), channel_id=1, replica_groups=mesh['dp'=16,'cls'=32] {'cls'}, use_global_device_ids=true, to_apply=%region_5.6 | all-reduce | flops 8192 | bytes 32768 | tf_op jit(solution)/shard_map/pmax | solution.py:56
  266.6 0.6 gather_fusion.1
  267.2 5.0 select_reduce_fusion
  272.2 0.9 convolution_bitcast_fusion
  273.0 0.9 convolution_bitcast_fusion.1
  273.9 0.0 all-reduce.4.cloned.1.call-start
  273.9 170.9 %all-reduce.6.cloned.1.call-done = (f32[64,128]{1,0:T(8,128)}, f32[64,128]{1,0:T(8,128)}) async-done(((f32[64,128]{1,0:T(8,128)}, f32[64,128]{1,0:T(8,128)}), (f32[64,128]{1,0:T(8,128)}, f32[64,128]{1,0:T(8,128)})) %all-reduce.6.cloned.1.call-update) | async-done | bytes 65552 | tf_op jit(solution)/shard_map/psum | solution.py:59
  444.9 1.4 subtract_bitcast_fusion
  446.3 0.6 gather_fusion.3
  446.9 7.6 %fusion.6 = f32[256,4,768]{0,2,1:T(8,128)} fusion(bf16[4,8,128,768]{3,2,1,0:T(8,128)(2,1)} %bitcast.47, f32[4,8,128,256]{3,2,1,0:T(8,128)} %get-tuple-element.22, f32[4,8,128]{2,1,0:T(8,128)S(1)} %bitcast.54, s32[4,8,256]{2,1,0:T(8,128)S(1)} %iota_add_fusion, s32[4,8,128]{2,1,0:T(8,128)S(1)} %bitcast.52, pred[4,8]{1,0:T(4,128)(4,1)S(1)} %broadcast_compare_fusion), kind=kOutput, calls=%fused_computation.14 | convolution fusion | flops 1617952768 | bytes 13697056 | tf_op jit(solution)/shard_map/jsit,jsid->tjd/dot_general | solution.py:79
  454.5 127.7 %all-reduce.4.cloned.1.call-done = f32[256,4,768]{0,2,1:T(8,128)} async-done(((f32[256,4,768]{0,2,1:T(8,128)}), f32[256,4,768]{0,2,1:T(8,128)}) %all-reduce.4.cloned.1.call-update) | async-done | bytes 3145744 | tf_op jit(solution)/shard_map/psum | solution.py:78
  582.2 1.9 constant_dynamic-slice_fusion
  584.1 1.1 copy.32
  (15 shorter events, 0.2 us)
Async XLA Ops:
  7.2 140.9 %copy-start = (bf16[4,256,768]{2,1,0:T(8,128)(2,1)S(1)}, bf16[4,256,768]{2,1,0:T(8,128)(2,1)}, u32[]{:S(2)}) copy-start(bf16[4,256,768]{2,1,0:T(8,128)(2,1)} %param.5) | copy-start | bytes 4718596
  7.2 132.8 %all-gather.4.cloned.1.call-start = ((), (), s32[]{:S(2)}) async-start(), calls=%async_computation | async-start | bytes 12976128 | tf_op jit(solution)/shard_map/all_gather | solution.py:12
  7.9 437.0 %all-reduce.6.cloned.1.call-start = ((), (), s32[]{:S(2)}) async-start(), calls=%async_computation.2 | async-start | bytes 131072 | tf_op jit(solution)/shard_map/psum | solution.py:59
  273.9 308.3 %all-reduce.4.cloned.1.call-start = ((), (), s32[]{:S(2)}) async-start(), calls=%async_computation.1 | async-start | bytes 6291456 | tf_op jit(solution)/shard_map/psum | solution.py:78
Sparse Core Ops, SparseCore 0:
  11.1 128.7 all-gather.3
  274.0 170.8 all-reduce.5
  454.6 127.5 all-reduce.3
where the time goes:
time: 592 us
  waiting for transfers between devices  366 us (62%)
  blocking collectives  176 us (30%)
  matrix products  15.9 us (3%)
  between operations  13.8 us (2%)
  local copies, waits for them, and re-layouts  13.4 us (2%)
  other arithmetic  7.47 us (1%)
    psum x1, waiting for transfers between devices, body(): lax.psum((jnp.einsum('bq,qi->bi', owner_float, jnp.sum(exp_weights, axis=...  171 us
    psum x1, waiting for transfers between devices, body(): lax.psum(jnp.einsum('jsit,jsid->tjd', logit_grad, image_tiles, preferred_...  128 us
    pmax x1, blocking collectives, body(): lax.pmax(local_max.astype(jnp.bfloat16), 'cls').astype(local_max.dtype)  112 us
    all_gather x1, waiting for transfers between devices, body(): lax.all_gather(embeddings, 'cls', axis=0, tiled=True)  66.1 us
    all_gather x1, blocking collectives, body(): lax.all_gather(cand_blocks, 'cls', axis=0, tiled=True)  33.4 us
    all_gather x1, blocking collectives, body(): lax.all_gather(label_pos, 'cls', axis=0, tiled=True)  30.6 us
  transfers between devices with their start and end apart: 3, of which 3 were waited for; matrix products, arithmetic and copies ran while one was open for 0% of the time, Pallas kernels for 0%

commit v1 on v0

--- a/solution.py
+++ b/solution.py
@@ -10,7 +10,9 @@
 def body(embeddings, class_rows, cand_blocks, label_pos):
     gathered, cand_all, labels_all = (
         lax.all_gather(embeddings, "cls", axis=0, tiled=True),
-        lax.all_gather(cand_blocks, "cls", axis=0, tiled=True),
+        jnp.concatenate(
+            lax.all_to_all(jnp.stack([cand_blocks] * lax.axis_size("cls")), "cls", 0, 0), axis=0
+        ),
         lax.all_gather(label_pos, "cls", axis=0, tiled=True),
     )
     local_blocks, block_taxa, feature_width = class_rows.shape

time: 592 us -> 592 us (level)
  blocking collectives: 176 us -> 145 us
  waiting for transfers between devices: 366 us -> 384 us
  starting transfers between devices: 0.12 us -> 10.6 us
    all_gather x1 -> x0, blocking collectives: 33.4 us -> none  [body(): lax.all_gather(cand_blocks, 'cls', axis=0, tiled=True)]
    all_gather x1, waiting for transfers between devices: 66.1 us -> 84.8 us  [body(): lax.all_gather(embeddings, 'cls', axis=0, tiled=True)]
    all_to_all x0 -> x1, starting transfers between devices: none -> 10.5 us  [body(): lax.all_to_all(jnp.stack([cand_blocks] * lax.axis_size('cls')), 'cls', 0, 0)]
  transfers between devices with their start and end apart: 3 -> 4, of which waited for: 3 -> 3; matrix products, arithmetic and copies ran while one was open for 0% -> 1% of each run, Pallas kernels for 0% -> 0%
where the time goes in v1:
time: 592 us
  waiting for transfers between devices  384 us (65%)
  blocking collectives  145 us (24%)
  matrix products  15.9 us (3%)
  local copies, waits for them, and re-layouts  14.7 us (2%)
  between operations  13.8 us (2%)
  starting transfers between devices  10.6 us (2%)
  other arithmetic  7.47 us (1%)
    psum x1, waiting for transfers between devices, body(): lax.psum((jnp.einsum('bq,qi->bi', owner_float, jnp.sum(exp_weights, axis=...  171 us
    psum x1, waiting for transfers between devices, body(): lax.psum(jnp.einsum('jsit,jsid->tjd', logit_grad, image_tiles, preferred_...  128 us
    pmax x1, blocking collectives, body(): lax.pmax(local_max.astype(jnp.bfloat16), 'cls').astype(local_max.dtype)  112 us
    all_gather x1, waiting for transfers between devices, body(): lax.all_gather(embeddings, 'cls', axis=0, tiled=True)  84.8 us
    all_gather x1, blocking collectives, body(): lax.all_gather(label_pos, 'cls', axis=0, tiled=True)  33.3 us
  transfers between devices with their start and end apart: 4, of which 3 were waited for; matrix products, arithmetic and copies ran while one was open for 1% of the time, Pallas kernels for 0%

profile of v1, /device:TPU:1, one launch (start us, length us, event | category | flops | bytes accessed | tf_op | source)
XLA Modules:
  0.0 591.5 jit_solution(16067459114633269120)
XLA Ops:
  7.2 0.7 all-gather.3.cloned.1.call-update
  7.9 1.3 stack.2
  9.2 10.5 %all-to-all-start = ((s32[32,2,8]{2,1,0:T(2,128)}), s32[32,2,8]{2,1,0:T(2,128)S(1)}, u32[]{:S(2)}, u32[]{:S(2)}) async-start(s32[32,2,8]{2,1,0:T(2,128)} %stack.2), calls=%async_computation | async-start | bytes 65536 | tf_op jit(solution)/shard_map/all_to_all | solution.py:14
  19.8 33.3 %all-gather = s32[32,1,256]{2,1,0:T(1,128)S(1)} all-gather(s32[1,1,256]{2,1,0:T(1,128)} %bitcast.55), channel_id=1, replica_groups=mesh['dp'=16,'cls'=32] {'cls'}, dimensions={0}, use_global_device_ids=true | all-gather | bytes 33792 | tf_op jit(solution)/shard_map/all_gather | solution.py:16
  53.1 0.1 eq.66
  53.2 0.1 copy.34
  53.3 0.1 fusion.10
  53.4 0.1 copy.35
  53.5 0.1 reduce_window_sum.11
  53.6 0.1 copy.36
  53.6 0.3 select_reduce_fusion.3
  54.0 0.1 reshape.116
  54.0 0.1 convert_compare_fusion
  54.1 0.1 copy.37
  54.2 0.6 gather_fusion.2
  54.8 0.1 iota_add_fusion
  54.9 84.8 %all-gather.3.cloned.1.call-done = bf16[8192,768]{1,0:T(8,128)(2,1)} async-done(((bf16[256,768]{1,0:T(8,128)(2,1)}), bf16[8192,768]{1,0:T(8,128)(2,1)}) %all-gather.3.cloned.1.call-update) | async-done | bytes 12582928 | tf_op jit(solution)/shard_map/all_gather | solution.py:12
  139.7 8.1 %gather_fusion = bf16[32,128,768]{2,1,0:T(8,128)(2,1)} fusion(bf16[64,128,768]{2,1,0:T(8,128)(2,1)} %bitcast.47, s32[1024]{0:T(1024)S(1)} %pad_clamp_fusion), kind=kCustom, calls=%fused_computation | custom fusion | bytes 12583040 | tf_op jit(solution)/shard_map/gather | solution.py:38
  147.9 6.5 %fusion.20 = (bf16[4,8,128]{2,1,0:T(8,128)(2,1)S(1)}, f32[4,8,128,256]{3,2,1,0:T(8,128)}) fusion(bf16[4,8,128,768]{3,2,1,0:T(8,128)(2,1)} %bitcast.45, bf16[4,256,768]{2,1,0:T(8,128)(2,1)S(1)} %copy-done), kind=kOutput, calls=%fused_computation.49 | convolution fusion | flops 1611657216 | bytes 12066816 | tf_op jit(solution)/shard_map/jsid,jtd->jsit/dot_general | solution.py:40
  154.4 0.4 select_reduce_fusion.2
  154.8 111.6 %pmax.7 = bf16[64,128]{1,0:T(8,128)(2,1)S(1)} all-reduce(bf16[64,128]{1,0:T(8,128)(2,1)S(1)} %select_reduce_fusion.2), channel_id=1, replica_groups=mesh['dp'=16,'cls'=32] {'cls'}, use_global_device_ids=true, to_apply=%region_5.6 | all-reduce | flops 8192 | bytes 32768 | tf_op jit(solution)/shard_map/pmax | solution.py:58
  266.4 0.6 gather_fusion.1
  267.0 5.0 select_reduce_fusion
  272.0 0.9 convolution_bitcast_fusion
  272.8 0.9 convolution_bitcast_fusion.1
  273.7 170.9 %all-reduce.6.cloned.1.call-done = (f32[64,128]{1,0:T(8,128)}, f32[64,128]{1,0:T(8,128)}) async-done(((f32[64,128]{1,0:T(8,128)}, f32[64,128]{1,0:T(8,128)}), (f32[64,128]{1,0:T(8,128)}, f32[64,128]{1,0:T(8,128)})) %all-reduce.6.cloned.1.call-update) | async-done | bytes 65552 | tf_op jit(solution)/shard_map/psum | solution.py:61
  444.6 1.4 subtract_bitcast_fusion
  446.0 0.6 gather_fusion.3
  446.6 7.6 %fusion.6 = f32[256,4,768]{0,2,1:T(8,128)} fusion(bf16[4,8,128,768]{3,2,1,0:T(8,128)(2,1)} %bitcast.46, f32[4,8,128,256]{3,2,1,0:T(8,128)} %get-tuple-element.24, f32[4,8,128]{2,1,0:T(8,128)S(1)} %bitcast.53, s32[4,8,256]{2,1,0:T(8,128)S(1)} %iota_add_fusion, s32[4,8,128]{2,1,0:T(8,128)S(1)} %bitcast.51, pred[4,8]{1,0:T(4,128)(4,1)S(1)} %broadcast_compare_fusion), kind=kOutput, calls=%fused_computation.14 | convolution fusion | flops 1617952768 | bytes 13697056 | tf_op jit(solution)/shard_map/jsit,jsid->tjd/dot_general | solution.py:81
  454.3 127.7 %all-reduce.4.cloned.1.call-done = f32[256,4,768]{0,2,1:T(8,128)} async-done(((f32[256,4,768]{0,2,1:T(8,128)}), f32[256,4,768]{0,2,1:T(8,128)}) %all-reduce.4.cloned.1.call-update) | async-done | bytes 3145744 | tf_op jit(solution)/shard_map/psum | solution.py:80
  582.0 1.9 constant_dynamic-slice_fusion
  583.9 1.1 copy.40
  (17 shorter events, 0.2 us)
Async XLA Ops:
  7.2 140.7 %copy-start = (bf16[4,256,768]{2,1,0:T(8,128)(2,1)S(1)}, bf16[4,256,768]{2,1,0:T(8,128)(2,1)}, u32[]{:S(2)}) copy-start(bf16[4,256,768]{2,1,0:T(8,128)(2,1)} %param.5) | copy-start | bytes 4718596
  7.2 132.6 %all-gather.3.cloned.1.call-start = ((), (), s32[]{:S(2)}) async-start(), calls=%async_computation.1 | async-start | bytes 12976128 | tf_op jit(solution)/shard_map/all_gather | solution.py:12
  9.2 44.0 %all-to-all-start = ((s32[32,2,8]{2,1,0:T(2,128)}), s32[32,2,8]{2,1,0:T(2,128)S(1)}, u32[]{:S(2)}, u32[]{:S(2)}) async-start(s32[32,2,8]{2,1,0:T(2,128)} %stack.2), calls=%async_computation | async-start | bytes 65536 | tf_op jit(solution)/shard_map/all_to_all | solution.py:14
  19.7 424.9 %all-reduce.6.cloned.1.call-start = ((), (), s32[]{:S(2)}) async-start(), calls=%async_computation.3 | async-start | bytes 131072 | tf_op jit(solution)/shard_map/psum | solution.py:61
  273.7 308.3 %all-reduce.4.cloned.1.call-start = ((), (), s32[]{:S(2)}) async-start(), calls=%async_computation.2 | async-start | bytes 6291456 | tf_op jit(solution)/shard_map/psum | solution.py:80
Sparse Core Ops, SparseCore 0:
  11.1 128.5 all-gather.2
  273.8 170.7 all-reduce.5
  454.4 127.5 all-reduce.3
